TPU v7x, 32 devices: a whole 2x2x4 slice. The times are simulated.
32 devices in a mesh: shots: 2 (over y), depth: 4 (over z), row: 4 (over x, core).
Axes of the slice: x: 2, y: 2, z: 4, core: 2. Of those that a mesh axis runs over, the one named last changes fastest.
Arguments:
- waves: float32 [8, 2, 512, 2, 1, 512], P(('shots', 'depth'), None, 'row'), parts along dimension 0, may hold values from -6 to 6
- slab_freq: float32 [8, 1], P(('shots', 'depth')), parts along dimension 0, may hold values from 1.2 to 2.4
- slowness: float32 [4, 512, 512], P('depth', 'row'), may hold values from 0.8 to 1.25
- ref_slow: float32 [4], P('depth'), may hold values from 0.9 to 1.1
- inj_freq: float32 [2, 1], P('shots'), parts along dimension 0, may hold values from 1.2 to 2.4
- wavelet: float32 [2, 1, 2], P('shots'), parts along dimension 0, may hold values from -64 to 64
- records: float32 [2, 1, 2, 4096], P('shots'), parts along dimension 0, may hold values from -6 to 6
- src_pos: int32 [4], P('shots'), parts along dimension 0, may hold values from 0 to 511
- rcv_pos: int32 [8192, 2], P('shots'), parts along dimension 0, may hold values from 0 to 511
Outputs:
- wave_out: float32 [8, 2, 512, 2, 1, 512], P(('shots', 'depth'), None, 'row'), parts along dimension 0
- image: float32 [8, 16, 512, 512], P(('shots', 'depth'), None, 'row'), parts along dimension 0
There are 2 independent parts, one for each index of `shots`. A program takes and returns all parts, laid end to end along the dimension named above; an argument that names none is the same for every part. Nothing has to cross between parts.
All inputs are finite; a program needn't handle non-finite values.
Results may differ from a plain program's by a relative error of at most 0.0003.
Values sent between devices are 32-bit elements; how exact they have to be, the bound alone decides.
A program may use at most 128 MiB of HBM per device.

v0:
```python
import functools
import math

import jax
import jax.numpy as jnp
import numpy as np
from jax import lax
from jax.experimental import pallas as pl
from jax.experimental.pallas import tpu as pltpu
from jax.sharding import PartitionSpec as P

OFF = 16
TICKS = 2
DZ = 4

MESH = pl.DeviceIdType.MESH
NT = (((1,), (1,)), ((), ()))
NN = (((1,), (0,)), ((), ()))


def half_tables(length):
    half = length // 2
    a = np.arange(half)
    mats = []
    for odd in (0, 1):
        turn = ((2 * a[:, None] + odd) * a[None, :]) % length
        angle = turn * (2.0 * math.pi / length)
        c, s = np.cos(angle), np.sin(angle)
        mats.append(np.block([[c, s], [-s, c]]))
    stacked = []
    for m in (mats[0], mats[1]):
        high = m.astype(np.float32).astype(jnp.bfloat16)
        low = (m - high.astype(np.float64)).astype(np.float32).astype(jnp.bfloat16)
        stacked += [high, low]
    return np.stack(stacked)


def split(value):
    high = value.astype(jnp.bfloat16)
    low = (value - high.astype(jnp.float32)).astype(jnp.bfloat16)
    return high, low


def dot(a, b, dims):
    return lax.dot_general(a, b, dims, preferred_element_type=jnp.float32)


def table_first(high, low, data):
    d_high, d_low = split(data)
    return dot(high, d_high, NT) + (dot(high, d_low, NT) + dot(low, d_high, NT))


def data_first(data, high, low):
    d_high, d_low = split(data)
    return dot(d_high, high, NN) + (dot(d_low, high, NN) + dot(d_high, low, NN))


def cos_sin(angle):
    turns = jnp.floor(angle * (2.0 / math.pi) + 0.5)
    r = angle - turns * 1.5703125
    r = r - turns * 4.837512969970703125e-4
    r = r - turns * 7.54978995489188216e-8
    z = r * r
    sine = r + r * z * (-1.6666654611e-1 + z * (8.3321608736e-3 + z * -1.9515295891e-4))
    cosine = 1.0 - 0.5 * z + z * z * (
        4.166664568298827e-2 + z * (-1.388731625493765e-3 + z * 2.443315711809948e-5)
    )
    quarter = turns.astype(jnp.int32)
    swap = (quarter & 1) == 1
    c = jnp.where(swap, sine, cosine)
    s = jnp.where(swap, cosine, sine)
    c = jnp.where(((quarter + 1) & 2) == 2, -c, c)
    s = jnp.where((quarter & 2) == 2, -s, s)
    return c, s


def kernel(
    n, depths, rows, cols, length, nrec,
    freq_ref, slow_ref, inj_ref, wavelet_ref, src_ref,
    waves_ref, table_ref, slowness_ref, pos_ref, rec_ref,
    shown_ref, image_out,
    u_first, image_ref, table_t, u_next, send1, recv1, send2, recv2, fld, phase, lens, freq_out, freq_in, hot,
    a2a_send, a2a_recv, z_send, z_recv, halo_send, halo_recv, f_send, f_recv, w_sem, i_sem, o_sem,
):
    half = length // 2
    wide = OFF // 2
    me = lax.axis_index("row")
    level = lax.axis_index("depth")
    deeper = level < depths - 1
    has_above = level > 0
    has_prev = me > 0
    has_next = me < n - 1

    def peer(off):
        return lax.rem(me + off, n)

    order = sorted(range(1, n), key=lambda off: abs(off - n / 2))

    def wave_copy(p, f):
        return pltpu.make_async_copy(waves_ref.at[p, :, f, 0, :], u_first.at[p, f], w_sem.at[p, f])

    def image_copy():
        return pltpu.make_async_copy(image_ref, image_out, i_sem)

    def shown_copy(f):
        return pltpu.make_async_copy(fld.at[TICKS - 1, :, f], shown_ref.at[:, f], o_sem.at[f])

    for f in (0, 1):
        for p in (0, 1):
            wave_copy(p, f).start()

    freq_out[...] = jnp.full(freq_out.shape, freq_ref[0, 0], jnp.float32)
    barrier = pltpu.get_barrier_semaphore()
    for off in order:
        pl.semaphore_signal(barrier, inc=1, device_id={"row": peer(off)}, device_id_type=MESH)

    @pl.when(deeper)
    def _():
        pl.semaphore_signal(barrier, inc=1, device_id={"depth": level + 1}, device_id_type=MESH)

    @pl.when(has_above)
    def _():
        pl.semaphore_signal(barrier, inc=1, device_id={"depth": level - 1}, device_id_type=MESH)

    sides = jnp.where(deeper, 1, 0) + jnp.where(has_above, 1, 0)
    pl.semaphore_wait(barrier, n - 1 + sides)

    below = lax.rem(level + 1, depths)

    def freq_copy():
        return pltpu.make_async_remote_copy(
            src_ref=freq_out, dst_ref=freq_in, send_sem=f_send, recv_sem=f_recv,
            device_id={"depth": below}, device_id_type=MESH)

    def z_copy(f):
        return pltpu.make_async_remote_copy(
            src_ref=fld.at[0, :, f, pl.ds(wide, rows), :], dst_ref=u_next.at[:, f],
            send_sem=z_send.at[f], recv_sem=z_recv.at[f],
            device_id={"depth": below}, device_id_type=MESH)

    def a2a1_copy(t, f, off):
        to = peer(off)
        return pltpu.make_async_remote_copy(
            src_ref=send1.at[t, f, pl.ds(pl.multiple_of(to * cols, cols), cols), :],
            dst_ref=recv1.at[t, f, me],
            send_sem=a2a_send.at[t, 0, f, off], recv_sem=a2a_recv.at[t, 0, f, off],
            device_id={"row": to}, device_id_type=MESH)

    def a2a2_copy(t, f, off):
        to = peer(off)
        return pltpu.make_async_remote_copy(
            src_ref=send2.at[t, f, pl.ds(pl.multiple_of(to * rows, rows), rows), :],
            dst_ref=recv2.at[t, f, me],
            send_sem=a2a_send.at[t, 1, f, off], recv_sem=a2a_recv.at[t, 1, f, off],
            device_id={"row": to}, device_id_type=MESH)

    def up_copy(t):
        return pltpu.make_async_remote_copy(
            src_ref=fld.at[t, :, :, pl.ds(rows, wide), :], dst_ref=fld.at[t, :, :, pl.ds(0, wide), :],
            send_sem=halo_send.at[t, 0], recv_sem=halo_recv.at[t, 0],
            device_id={"row": peer(1)}, device_id_type=MESH)

    def down_copy(t):
        return pltpu.make_async_remote_copy(
            src_ref=fld.at[t, :, :, pl.ds(wide, wide), :],
            dst_ref=fld.at[t, :, :, pl.ds(rows + wide, wide), :],
            send_sem=halo_send.at[t, 1], recv_sem=halo_recv.at[t, 1],
            device_id={"row": peer(n - 1)}, device_id_type=MESH)

    @pl.when(deeper)
    def _():
        freq_copy().start()

    def forward_y(t, f, real, imag):
        for parity in (0, 1):
            if parity == 0:
                folded = jnp.concatenate(
                    [real[:, :half] + real[:, half:], imag[:, :half] + imag[:, half:]], axis=1)
            else:
                folded = jnp.concatenate(
                    [real[:, :half] - real[:, half:], imag[:, :half] - imag[:, half:]], axis=1)
            result = table_first(table_ref[2 * parity], table_ref[2 * parity + 1], folded)
            send1[t, f, pl.ds(parity * half, half), pl.ds(0, rows)] = result[:half]
            send1[t, f, pl.ds(parity * half, half), pl.ds(rows, rows)] = result[half:]
        for off in order:
            a2a1_copy(t, f, off).start()
        recv1[t, f, me] = send1[t, f, pl.ds(pl.multiple_of(me * cols, cols), cols), :]

    def middle(t, f):
        for off in order:
            a2a1_copy(t, f, off).wait_recv()
        sign = 1.0 if f == 0 else -1.0
        real = jnp.concatenate([recv1[t, f, s, :, pl.ds(0, rows)] for s in range(n)], axis=1)
        imag = jnp.concatenate([recv1[t, f, s, :, pl.ds(rows, rows)] for s in range(n)], axis=1)
        results = []
        for parity in (0, 1):
            if parity == 0:
                folded = jnp.concatenate(
                    [real[:, :half] + real[:, half:], imag[:, :half] + imag[:, half:]], axis=1)
            else:
                folded = jnp.concatenate(
                    [real[:, :half] - real[:, half:], imag[:, :half] - imag[:, half:]], axis=1)
            spectrum = data_first(folded, table_t[2 * parity], table_t[2 * parity + 1])
            p_real = phase[t, 0, :, pl.ds(parity * half, half)]
            p_imag = phase[t, 1, :, pl.ds(parity * half, half)] * sign
            s_real, s_imag = spectrum[:, :half], spectrum[:, half:]
            shifted = jnp.concatenate(
                [s_real * p_real - s_imag * p_imag, s_real * p_imag + s_imag * p_real], axis=1)
            results.append(table_first(table_t[2 * parity], table_t[2 * parity + 1], shifted))
        total = results[0] + results[1]
        send2[t, f, pl.ds(0, half), pl.ds(0, cols)] = total[:half]
        send2[t, f, pl.ds(0, half), pl.ds(cols, cols)] = total[half:]
        total = results[0] - results[1]
        send2[t, f, pl.ds(half, half), pl.ds(0, cols)] = total[:half]
        send2[t, f, pl.ds(half, half), pl.ds(cols, cols)] = total[half:]
        for off in order:
            a2a2_copy(t, f, off).start()
        recv2[t, f, me] = send2[t, f, pl.ds(pl.multiple_of(me * rows, rows), rows), :]

    def inverse_y(t, f):
        for off in order:
            a2a2_copy(t, f, off).wait_recv()
        sign = 1.0 if f == 0 else -1.0
        real = jnp.concatenate([recv2[t, f, s, :, pl.ds(0, cols)] for s in range(n)], axis=1)
        imag = jnp.concatenate([recv2[t, f, s, :, pl.ds(cols, cols)] for s in range(n)], axis=1)
        even = data_first(
            jnp.concatenate([real[:, :half], imag[:, :half]], axis=1), table_ref[0], table_ref[1])
        odd = data_first(
            jnp.concatenate([real[:, half:], imag[:, half:]], axis=1), table_ref[2], table_ref[3])
        for part in (0, 1):
            total = even + odd if part == 0 else even - odd
            window = pl.ds(part * half, half)
            l_cos = lens[t, 0, :, window]
            l_sin = lens[t, 1, :, window] * sign
            t_real, t_imag = total[:, :half], total[:, half:]
            fld[t, 0, f, pl.ds(wide, rows), window] = t_real * l_cos - t_imag * l_sin
            fld[t, 1, f, pl.ds(wide, rows), window] = t_real * l_sin + t_imag * l_cos

    def wave_number(index):
        order_of = jnp.where(index < half, 2 * index, 2 * (index - half) + 1)
        signed = jnp.where(order_of < half, order_of, order_of - length)
        k = signed.astype(jnp.float32) * (2.0 * math.pi / length)
        return k * k

    def factors(t, freq):
        ref_slow = slow_ref[0]
        number = freq * ref_slow
        block = min(cols, 32)

        def phase_block(i, carry):
            base = pl.multiple_of(i * block, block)
            ky = wave_number(lax.broadcasted_iota(jnp.int32, (block, length), 0) + (me * cols + base))
            kx = wave_number(lax.broadcasted_iota(jnp.int32, (block, length), 1))
            vertical = number * number - (kx + ky)
            root = jnp.sqrt(jnp.abs(vertical)) * float(DZ)
            moving = vertical > 0
            c, s = cos_sin(root)
            scale = 1.0 / (length * length)
            phase[t, 0, pl.ds(base, block), :] = jnp.where(moving, c, jnp.exp(-root)) * scale
            phase[t, 1, pl.ds(base, block), :] = jnp.where(moving, s, 0.0) * scale
            return carry

        lax.fori_loop(0, cols // block, phase_block, 0)
        block_r = min(rows, 32)

        def lens_block(i, carry):
            base = pl.multiple_of(i * block_r, block_r)
            angle = freq * (slowness_ref[pl.ds(base, block_r), :] - ref_slow) * float(DZ)
            c, s = cos_sin(angle)
            lens[t, 0, pl.ds(base, block_r), :] = c
            lens[t, 1, pl.ds(base, block_r), :] = s
            return carry

        lax.fori_loop(0, rows // block_r, lens_block, 0)

    def inject():
        row_ids = lax.broadcasted_iota(jnp.int32, (rows, 1), 0) + me * rows
        col_ids = lax.broadcasted_iota(jnp.int32, (1, length), 1)
        point = (row_ids == src_ref[0]) & (col_ids == src_ref[1])
        for p in (0, 1):
            u_next[p, 0] = jnp.where(point, wavelet_ref[0, p], 0.0)
        chunk = min(512, nrec)

        def step(i, carry):
            base = pl.multiple_of(i * chunk, chunk)
            x = pos_ref[pl.ds(0, 1), pl.ds(base, chunk)]
            y = pos_ref[pl.ds(1, 1), pl.ds(base, chunk)]
            in_row = lax.broadcasted_iota(jnp.int32, (rows, chunk), 0) + me * rows == x
            in_col = jnp.where(
                lax.broadcasted_iota(jnp.int32, (length, chunk), 0) == y, 1.0, 0.0).astype(jnp.bfloat16)
            parts = []
            for p in (0, 1):
                value = rec_ref[pl.ds(p, 1), pl.ds(base, chunk)]
                parts.append(jnp.where(in_row, value, 0.0))
            left = jnp.concatenate(parts, axis=0)
            high, low = split(left)
            added = dot(high, in_col, NT) + dot(low, in_col, NT)
            hot[...] = hot[...] + added
            return carry

        hot[...] = jnp.zeros_like(hot)
        lax.fori_loop(0, nrec // chunk, step, 0)
        u_next[0, 1] = hot[pl.ds(0, rows), :]
        u_next[1, 1] = hot[pl.ds(rows, rows), :]

    def halo_start(t):
        zero = jnp.zeros((2, 2, wide, length), jnp.float32)

        @pl.when(has_next)
        def _():
            up_copy(t).start()

        @pl.when(has_prev)
        def _():
            down_copy(t).start()

        @pl.when(jnp.logical_not(has_prev))
        def _():
            fld[t, :, :, pl.ds(0, wide), :] = zero

        @pl.when(jnp.logical_not(has_next))
        def _():
            fld[t, :, :, pl.ds(rows + wide, wide), :] = zero

    def halo_wait(t):
        @pl.when(has_prev)
        def _():
            up_copy(t).wait_recv()

        @pl.when(has_next)
        def _():
            down_copy(t).wait_recv()

    def imaging(t):
        def block(i, carry):
            base = pl.multiple_of(i * 8, 8)
            window = pl.ds(base, 8 + 2 * wide)
            values = [fld[t, p, f, window, :] for f in (0, 1) for p in (0, 1)]
            for j in range(OFF):
                h = j - wide
                s_real, s_imag = (v[wide - h:wide - h + 8] for v in values[:2])
                r_real, r_imag = (v[wide + h:wide + h + 8] for v in values[2:])
                term = s_real * r_real + s_imag * r_imag
                image_ref[j, pl.ds(base, 8), :] = term
            return carry

        lax.fori_loop(0, rows // 8, block, 0)

    for f in (0, 1):
        for p in (0, 1):
            wave_copy(p, f).wait()
        forward_y(0, f, u_first[0, f], u_first[1, f])
    for i in range(4):
        table_t[i] = table_ref[i].T
    factors(0, freq_ref[0, 0])
    for f in (0, 1):
        middle(0, f)

    @pl.when(jnp.logical_not(has_above))
    def _():
        factors(1, inj_ref[0, 0])

    @pl.when(has_above)
    def _():
        freq_copy().wait_recv()
        factors(1, freq_in[pl.ds(0, 1), pl.ds(0, 1)])

    for f in (0, 1):
        inverse_y(0, f)

        @pl.when(deeper)
        def _():
            z_copy(f).start()

    halo_start(0)

    @pl.when(jnp.logical_not(has_above))
    def _():
        inject()

    halo_wait(0)
    imaging(0)
    image_copy().start()

    for f in (0, 1):
        @pl.when(has_above)
        def _():
            z_copy(f).wait_recv()

        forward_y(1, f, u_next[0, f], u_next[1, f])
    for f in (0, 1):
        middle(1, f)
    for f in (0, 1):
        inverse_y(1, f)
    halo_start(1)
    halo_wait(1)
    for f in (0, 1):
        shown_copy(f).start()
    for t in range(TICKS):
        for f in (0, 1):
            for off in order:
                a2a1_copy(t, f, off).wait_send()
                a2a2_copy(t, f, off).wait_send()

        @pl.when(has_next)
        def _():
            up_copy(t).wait_send()

        @pl.when(has_prev)
        def _():
            down_copy(t).wait_send()

    @pl.when(deeper)
    def _():
        freq_copy().wait_send()
        for f in (0, 1):
            z_copy(f).wait_send()

    image_copy().wait()
    for f in (0, 1):
        shown_copy(f).wait()


def finish(rows, length, fld_ref, before_ref, out_ref, image_ref, o_sem):
    wide = OFF // 2
    step = pl.program_id(0)
    block = image_ref.shape[1]

    def out_copy(p, f):
        return pltpu.make_async_copy(
            fld_ref.at[p, f, pl.ds(wide, rows), :], out_ref.at[p, :, f, 0, :], o_sem.at[p, f])

    @pl.when(step == 0)
    def _():
        for f in (0, 1):
            for p in (0, 1):
                out_copy(p, f).start()

    def part(i, carry):
        base = pl.multiple_of(i * 8, 8)
        window = pl.ds(pl.multiple_of(step * block + base, 8), 8 + 2 * wide)
        values = [fld_ref[p, f, window, :] for f in (0, 1) for p in (0, 1)]
        for j in range(OFF):
            h = j - wide
            s_real, s_imag = (v[wide - h:wide - h + 8] for v in values[:2])
            r_real, r_imag = (v[wide + h:wide + h + 8] for v in values[2:])
            term = s_real * r_real + s_imag * r_imag
            image_ref[j, pl.ds(base, 8), :] = before_ref[j, pl.ds(base, 8), :] + term
        return carry

    lax.fori_loop(0, block // 8, part, 0)

    @pl.when(step == pl.num_programs(0) - 1)
    def _():
        for f in (0, 1):
            for p in (0, 1):
                out_copy(p, f).wait()


def solution(mesh):
    n, depths = mesh.shape["row"], mesh.shape["depth"]

    def local(waves, slab_freq, slowness, ref_slow, inj_freq, wavelet, records, src_pos, rcv_pos):
        rows, length = waves.shape[2], waves.shape[5]
        cols = length // n
        nrec = rcv_pos.shape[0]
        assert waves.shape[4] == 1 and slowness.shape[0] == 1
        assert inj_freq.shape[0] == TICKS - 1
        table = jnp.asarray(half_tables(length), jnp.bfloat16)
        vmem = pl.BlockSpec(memory_space=pltpu.VMEM)
        smem = pl.BlockSpec(memory_space=pltpu.SMEM)
        f32 = jnp.float32
        hbm = pl.BlockSpec(memory_space=pl.ANY)
        shown, before = pl.pallas_call(
            functools.partial(kernel, n, depths, rows, cols, length, nrec),
            out_shape=(
                jax.ShapeDtypeStruct((2, 2, rows + OFF, length), f32),
                jax.ShapeDtypeStruct((OFF, rows, length), f32),
            ),
            in_specs=[smem] * 5 + [hbm] + [vmem] * 4,
            out_specs=(hbm, hbm),
            scratch_shapes=[
                pltpu.VMEM((2, 2, rows, length), f32),
                pltpu.VMEM((OFF, rows, length), f32),
                pltpu.VMEM((4, length, length), jnp.bfloat16),
                pltpu.VMEM((2, 2, rows, length), f32),
                pltpu.VMEM((TICKS, 2, length, 2 * rows), f32),
                pltpu.VMEM((TICKS, 2, n, cols, 2 * rows), f32),
                pltpu.VMEM((TICKS, 2, length, 2 * cols), f32),
                pltpu.VMEM((TICKS, 2, n, rows, 2 * cols), f32),
                pltpu.VMEM((TICKS, 2, 2, rows + OFF, length), f32),
                pltpu.VMEM((TICKS, 2, cols, length), f32),
                pltpu.VMEM((TICKS, 2, rows, length), f32),
                pltpu.VMEM((8, 128), f32),
                pltpu.VMEM((8, 128), f32),
                pltpu.VMEM((2 * rows, length), f32),
                pltpu.SemaphoreType.DMA((TICKS, 2, 2, n)),
                pltpu.SemaphoreType.DMA((TICKS, 2, 2, n)),
                pltpu.SemaphoreType.DMA((2,)),
                pltpu.SemaphoreType.DMA((2,)),
                pltpu.SemaphoreType.DMA((TICKS, 2)),
                pltpu.SemaphoreType.DMA((TICKS, 2)),
                pltpu.SemaphoreType.DMA,
                pltpu.SemaphoreType.DMA,
                pltpu.SemaphoreType.DMA((2, 2)),
                pltpu.SemaphoreType.DMA,
                pltpu.SemaphoreType.DMA((2,)),
            ],
            compiler_params=pltpu.CompilerParams(
                collective_id=0, has_side_effects=True, vmem_limit_bytes=60 * 2**20
            ),
        )(
            slab_freq, ref_slow, inj_freq, wavelet[0], src_pos,
            waves.reshape(2, rows, 2, 1, length), table, slowness[0], rcv_pos.T, records[0, 0],
        )
        block = min(rows, 16)
        out, image = pl.pallas_call(
            functools.partial(finish, rows, length),
            grid=(rows // block,),
            out_shape=(
                jax.ShapeDtypeStruct((2, rows, 2, 1, length), f32),
                jax.ShapeDtypeStruct((OFF, rows, length), f32),
            ),
            in_specs=[
                pl.BlockSpec((2, 2, rows + OFF, length), lambda i: (0, 0, 0, 0)),
                pl.BlockSpec((OFF, block, length), lambda i: (0, i, 0)),
            ],
            out_specs=(hbm, pl.BlockSpec((OFF, block, length), lambda i: (0, i, 0))),
            scratch_shapes=[pltpu.SemaphoreType.DMA((2, 2))],
            compiler_params=pltpu.CompilerParams(vmem_limit_bytes=60 * 2**20),
        )(shown, before)
        return out.reshape(1, 2, rows, 2, 1, length), image[None]

    placed = (
        P(("shots", "depth"), None, "row", None, None, None),
        P(("shots", "depth"), None),
        P("depth", "row", None),
        P("depth"),
        P("shots", None),
        P("shots", None, None),
        P("shots", None, None, None),
        P("shots"),
        P("shots", None),
    )
    return jax.shard_map(
        local,
        mesh=mesh,
        in_specs=placed,
        out_specs=(
            P(("shots", "depth"), None, "row", None, None, None),
            P(("shots", "depth"), None, "row", None),
        ),
        check_vma=False,
    )
```

profile of v0, /device:TPU:13, one launch (start us, length us, event | category | flops | bytes accessed | tf_op | source)
XLA Modules:
  0.0 82.2 jit_solution(6464340916032154653)
XLA Ops:
  2.6 71.8 %shard_map.113 = (f32[2,2,144,512]{3,2,1,0:T(8,128)}, f32[16,128,512]{2,1,0:T(8,128)}) custom-call(f32[1,1]{1,0:T(1,128)S(6)} %copy.12.freq_ref, f32[1]{0:T(128)S(6)} %copy.13.slow_ref, f32[1,1]{1,0:T(1,128)S(6)} %copy.14.inj_ref, f32[1,2]{1,0:T(1,128)} %bitcast.11, s32[2]{0:T(128)} %src_ref.1, f32[2,128,2,1,512]{4,3,2,1,0:T(1,128)} %bitcast.7, ...), custom_call_target="tpu_custom_call" | custom-call | tf_op jit(solution)/shard_map/pallas_call | solution.py:474
  74.4 7.8 %shard_map.114 = (f32[2,128,2,1,512]{4,3,2,1,0:T(1,128)}, f32[16,128,512]{2,1,0:T(8,128)}) custom-call(f32[2,2,144,512]{3,2,1,0:T(8,128)} %get-tuple-element.6.fld_ref, f32[16,128,512]{2,1,0:T(8,128)} %get-tuple-element.7.before_ref), custom_call_target="tpu_custom_call" | custom-call | tf_op jit(solution)/shard_map/pallas_call | solution.py:517
where the time goes:
time: 82.5 us; the launch traced here: 82.2 us
  Pallas kernels  79.6 us (96%)
  between operations  2.58 us (3%)
    pallas_call x1, Pallas kernels, local(): pl.pallas_call(functools.partial(kernel, n, depths, rows, cols, length, n...  71.8 us
    pallas_call x1, Pallas kernels, local(): pl.pallas_call(functools.partial(finish, rows, length), grid=(rows // blo...  7.78 us

commit v1 on v0

--- a/solution.py
+++ b/solution.py
@@ -75,15 +75,17 @@
 
 
 def kernel(
-    n, depths, rows, cols, length, nrec,
+    n, depths, rows, cols, length, nrec, parts,
     freq_ref, slow_ref, inj_ref, wavelet_ref, src_ref,
     waves_ref, table_ref, slowness_ref, pos_ref, rec_ref,
     shown_ref, image_out,
-    u_first, image_ref, table_t, u_next, send1, recv1, send2, recv2, fld, phase, lens, freq_out, freq_in, hot,
+    u_first, image_ref, table_t, table_x, u_next, send1, recv1, send2, recv2, fld, phase, lens, freq_out, freq_in, hot,
     a2a_send, a2a_recv, z_send, z_recv, halo_send, halo_recv, f_send, f_recv, w_sem, i_sem, o_sem,
 ):
     half = length // 2
     wide = OFF // 2
+    piece = rows // parts
+    tiles = length // 128
     me = lax.axis_index("row")
     level = lax.axis_index("depth")
     deeper = level < depths - 1
@@ -132,38 +134,40 @@
             src_ref=freq_out, dst_ref=freq_in, send_sem=f_send, recv_sem=f_recv,
             device_id={"depth": below}, device_id_type=MESH)
 
-    def z_copy(f):
+    def z_copy(f, part):
         return pltpu.make_async_remote_copy(
-            src_ref=fld.at[0, :, f, pl.ds(wide, rows), :], dst_ref=u_next.at[:, f],
-            send_sem=z_send.at[f], recv_sem=z_recv.at[f],
+            src_ref=fld.at[0, :, f, :, pl.ds(wide + part * piece, piece), :],
+            dst_ref=u_next.at[:, f, :, pl.ds(part * piece, piece), :],
+            send_sem=z_send.at[f, part], recv_sem=z_recv.at[f, part],
             device_id={"depth": below}, device_id_type=MESH)
 
-    def a2a1_copy(t, f, off):
+    def a2a1_copy(t, f, part, off):
         to = peer(off)
         return pltpu.make_async_remote_copy(
-            src_ref=send1.at[t, f, pl.ds(pl.multiple_of(to * cols, cols), cols), :],
-            dst_ref=recv1.at[t, f, me],
-            send_sem=a2a_send.at[t, 0, f, off], recv_sem=a2a_recv.at[t, 0, f, off],
+            src_ref=send1.at[t, f, part, pl.ds(pl.multiple_of(to * cols, cols), cols), :],
+            dst_ref=recv1.at[t, f, part, me],
+            send_sem=a2a_send.at[t, 0, f, part, off], recv_sem=a2a_recv.at[t, 0, f, part, off],
             device_id={"row": to}, device_id_type=MESH)
 
-    def a2a2_copy(t, f, off):
+    def a2a2_copy(t, f, part, off):
         to = peer(off)
+        first = pl.multiple_of(to * rows + part * piece, piece)
         return pltpu.make_async_remote_copy(
-            src_ref=send2.at[t, f, pl.ds(pl.multiple_of(to * rows, rows), rows), :],
-            dst_ref=recv2.at[t, f, me],
-            send_sem=a2a_send.at[t, 1, f, off], recv_sem=a2a_recv.at[t, 1, f, off],
+            src_ref=send2.at[t, f, pl.ds(first, piece), :],
+            dst_ref=recv2.at[t, f, me, pl.ds(part * piece, piece), :],
+            send_sem=a2a_send.at[t, 1, f, part, off], recv_sem=a2a_recv.at[t, 1, f, part, off],
             device_id={"row": to}, device_id_type=MESH)
 
     def up_copy(t):
         return pltpu.make_async_remote_copy(
-            src_ref=fld.at[t, :, :, pl.ds(rows, wide), :], dst_ref=fld.at[t, :, :, pl.ds(0, wide), :],
+            src_ref=fld.at[t, :, :, :, pl.ds(rows, wide), :], dst_ref=fld.at[t, :, :, :, pl.ds(0, wide), :],
             send_sem=halo_send.at[t, 0], recv_sem=halo_recv.at[t, 0],
             device_id={"row": peer(1)}, device_id_type=MESH)
 
     def down_copy(t):
         return pltpu.make_async_remote_copy(
-            src_ref=fld.at[t, :, :, pl.ds(wide, wide), :],
-            dst_ref=fld.at[t, :, :, pl.ds(rows + wide, wide), :],
+            src_ref=fld.at[t, :, :, :, pl.ds(wide, wide), :],
+            dst_ref=fld.at[t, :, :, :, pl.ds(rows + wide, wide), :],
             send_sem=halo_send.at[t, 1], recv_sem=halo_recv.at[t, 1],
             device_id={"row": peer(n - 1)}, device_id_type=MESH)
 
@@ -171,7 +175,7 @@
     def _():
         freq_copy().start()
 
-    def forward_y(t, f, real, imag):
+    def forward_y(t, f, part, real, imag):
         for parity in (0, 1):
             if parity == 0:
                 folded = jnp.concatenate(
@@ -180,27 +184,44 @@
                 folded = jnp.concatenate(
                     [real[:, :half] - real[:, half:], imag[:, :half] - imag[:, half:]], axis=1)
             result = table_first(table_ref[2 * parity], table_ref[2 * parity + 1], folded)
-            send1[t, f, pl.ds(parity * half, half), pl.ds(0, rows)] = result[:half]
-            send1[t, f, pl.ds(parity * half, half), pl.ds(rows, rows)] = result[half:]
+            send1[t, f, part, pl.ds(parity * half, half), pl.ds(0, piece)] = result[:half]
+            send1[t, f, part, pl.ds(parity * half, half), pl.ds(piece, piece)] = result[half:]
         for off in order:
-            a2a1_copy(t, f, off).start()
-        recv1[t, f, me] = send1[t, f, pl.ds(pl.multiple_of(me * cols, cols), cols), :]
+            a2a1_copy(t, f, part, off).start()
+        recv1[t, f, part, me] = send1[t, f, part, pl.ds(pl.multiple_of(me * cols, cols), cols), :]
+
+    def next_field(part):
+        window = pl.ds(part * piece, piece)
+
+        def read(f):
+            return [
+                jnp.concatenate([u_next[p, f, i, window, :] for i in range(tiles)], axis=1)
+                for p in (0, 1)
+            ]
+
+        return read
+
+    def forward_next(f, part):
+        @pl.when(has_above)
+        def _():
+            z_copy(f, part).wait_recv()
+
+        forward_y(1, f, part, *next_field(part)(f))
 
     def middle(t, f):
-        for off in order:
-            a2a1_copy(t, f, off).wait_recv()
+        for part in range(parts):
+            for off in order:
+                a2a1_copy(t, f, part, off).wait_recv()
         sign = 1.0 if f == 0 else -1.0
-        real = jnp.concatenate([recv1[t, f, s, :, pl.ds(0, rows)] for s in range(n)], axis=1)
-        imag = jnp.concatenate([recv1[t, f, s, :, pl.ds(rows, rows)] for s in range(n)], axis=1)
+        pairs = [(s, part) for s in range(n // 2) for part in range(parts)]
         results = []
         for parity in (0, 1):
-            if parity == 0:
-                folded = jnp.concatenate(
-                    [real[:, :half] + real[:, half:], imag[:, :half] + imag[:, half:]], axis=1)
-            else:
-                folded = jnp.concatenate(
-                    [real[:, :half] - real[:, half:], imag[:, :half] - imag[:, half:]], axis=1)
-            spectrum = data_first(folded, table_t[2 * parity], table_t[2 * parity + 1])
+            pieces = []
+            for s, part in pairs:
+                near, far = recv1[t, f, part, s], recv1[t, f, part, s + n // 2]
+                pieces.append(near + far if parity == 0 else near - far)
+            folded = jnp.concatenate(pieces, axis=1)
+            spectrum = data_first(folded, table_x[2 * parity], table_x[2 * parity + 1])
             p_real = phase[t, 0, :, pl.ds(parity * half, half)]
             p_imag = phase[t, 1, :, pl.ds(parity * half, half)] * sign
             s_real, s_imag = spectrum[:, :half], spectrum[:, half:]
@@ -213,28 +234,35 @@
         total = results[0] - results[1]
         send2[t, f, pl.ds(half, half), pl.ds(0, cols)] = total[:half]
         send2[t, f, pl.ds(half, half), pl.ds(cols, cols)] = total[half:]
+        for part in range(parts):
+            for off in order:
+                a2a2_copy(t, f, part, off).start()
+        recv2[t, f, me] = send2[t, f, pl.ds(pl.multiple_of(me * rows, rows), rows), :]
+
+    def inverse_y(t, f, part):
         for off in order:
-            a2a2_copy(t, f, off).start()
-        recv2[t, f, me] = send2[t, f, pl.ds(pl.multiple_of(me * rows, rows), rows), :]
-
-    def inverse_y(t, f):
-        for off in order:
-            a2a2_copy(t, f, off).wait_recv()
+            a2a2_copy(t, f, part, off).wait_recv()
         sign = 1.0 if f == 0 else -1.0
-        real = jnp.concatenate([recv2[t, f, s, :, pl.ds(0, cols)] for s in range(n)], axis=1)
-        imag = jnp.concatenate([recv2[t, f, s, :, pl.ds(cols, cols)] for s in range(n)], axis=1)
+        span = pl.ds(part * piece, piece)
+        real = jnp.concatenate([recv2[t, f, s, span, pl.ds(0, cols)] for s in range(n)], axis=1)
+        imag = jnp.concatenate([recv2[t, f, s, span, pl.ds(cols, cols)] for s in range(n)], axis=1)
         even = data_first(
             jnp.concatenate([real[:, :half], imag[:, :half]], axis=1), table_ref[0], table_ref[1])
         odd = data_first(
             jnp.concatenate([real[:, half:], imag[:, half:]], axis=1), table_ref[2], table_ref[3])
-        for part in (0, 1):
-            total = even + odd if part == 0 else even - odd
-            window = pl.ds(part * half, half)
-            l_cos = lens[t, 0, :, window]
-            l_sin = lens[t, 1, :, window] * sign
+        for side in (0, 1):
+            total = even + odd if side == 0 else even - odd
+            window = pl.ds(side * half, half)
+            l_cos = lens[t, 0, span, window]
+            l_sin = lens[t, 1, span, window] * sign
             t_real, t_imag = total[:, :half], total[:, half:]
-            fld[t, 0, f, pl.ds(wide, rows), window] = t_real * l_cos - t_imag * l_sin
-            fld[t, 1, f, pl.ds(wide, rows), window] = t_real * l_sin + t_imag * l_cos
+            new_real = t_real * l_cos - t_imag * l_sin
+            new_imag = t_real * l_sin + t_imag * l_cos
+            inner = pl.ds(wide + part * piece, piece)
+            for i in range(half // 128):
+                lanes = slice(i * 128, (i + 1) * 128)
+                fld[t, 0, f, side * (half // 128) + i, inner, :] = new_real[:, lanes]
+                fld[t, 1, f, side * (half // 128) + i, inner, :] = new_imag[:, lanes]
 
     def wave_number(index):
         order_of = jnp.where(index < half, 2 * index, 2 * (index - half) + 1)
@@ -278,7 +306,9 @@
         col_ids = lax.broadcasted_iota(jnp.int32, (1, length), 1)
         point = (row_ids == src_ref[0]) & (col_ids == src_ref[1])
         for p in (0, 1):
-            u_next[p, 0] = jnp.where(point, wavelet_ref[0, p], 0.0)
+            source = jnp.where(point, wavelet_ref[0, p], 0.0)
+            for i in range(tiles):
+                u_next[p, 0, i] = source[:, i * 128:(i + 1) * 128]
         chunk = min(512, nrec)
 
         def step(i, carry):
@@ -288,11 +318,11 @@
             in_row = lax.broadcasted_iota(jnp.int32, (rows, chunk), 0) + me * rows == x
             in_col = jnp.where(
                 lax.broadcasted_iota(jnp.int32, (length, chunk), 0) == y, 1.0, 0.0).astype(jnp.bfloat16)
-            parts = []
+            both = []
             for p in (0, 1):
                 value = rec_ref[pl.ds(p, 1), pl.ds(base, chunk)]
-                parts.append(jnp.where(in_row, value, 0.0))
-            left = jnp.concatenate(parts, axis=0)
+                both.append(jnp.where(in_row, value, 0.0))
+            left = jnp.concatenate(both, axis=0)
             high, low = split(left)
             added = dot(high, in_col, NT) + dot(low, in_col, NT)
             hot[...] = hot[...] + added
@@ -300,11 +330,12 @@
 
         hot[...] = jnp.zeros_like(hot)
         lax.fori_loop(0, nrec // chunk, step, 0)
-        u_next[0, 1] = hot[pl.ds(0, rows), :]
-        u_next[1, 1] = hot[pl.ds(rows, rows), :]
+        for p in (0, 1):
+            for i in range(tiles):
+                u_next[p, 1, i] = hot[pl.ds(p * rows, rows), pl.ds(i * 128, 128)]
 
     def halo_start(t):
-        zero = jnp.zeros((2, 2, wide, length), jnp.float32)
+        zero = jnp.zeros((2, 2, tiles, wide, 128), jnp.float32)
 
         @pl.when(has_next)
         def _():
@@ -316,11 +347,11 @@
 
         @pl.when(jnp.logical_not(has_prev))
         def _():
-            fld[t, :, :, pl.ds(0, wide), :] = zero
+            fld[t, :, :, :, pl.ds(0, wide), :] = zero
 
         @pl.when(jnp.logical_not(has_next))
         def _():
-            fld[t, :, :, pl.ds(rows + wide, wide), :] = zero
+            fld[t, :, :, :, pl.ds(rows + wide, wide), :] = zero
 
     def halo_wait(t):
         @pl.when(has_prev)
@@ -334,14 +365,13 @@
     def imaging(t):
         def block(i, carry):
             base = pl.multiple_of(i * 8, 8)
-            window = pl.ds(base, 8 + 2 * wide)
-            values = [fld[t, p, f, window, :] for f in (0, 1) for p in (0, 1)]
-            for j in range(OFF):
-                h = j - wide
-                s_real, s_imag = (v[wide - h:wide - h + 8] for v in values[:2])
-                r_real, r_imag = (v[wide + h:wide + h + 8] for v in values[2:])
-                term = s_real * r_real + s_imag * r_imag
-                image_ref[j, pl.ds(base, 8), :] = term
+            for i_tile in range(tiles):
+                for j in range(OFF):
+                    h = j - wide
+                    behind, ahead = pl.ds(base + (wide - h), 8), pl.ds(base + (wide + h), 8)
+                    image_ref[j, pl.ds(base, 8), pl.ds(i_tile * 128, 128)] = (
+                        fld[t, 0, 0, i_tile, behind, :] * fld[t, 0, 1, i_tile, ahead, :]
+                        + fld[t, 1, 0, i_tile, behind, :] * fld[t, 1, 1, i_tile, ahead, :])
             return carry
 
         lax.fori_loop(0, rows // 8, block, 0)
@@ -349,12 +379,21 @@
     for f in (0, 1):
         for p in (0, 1):
             wave_copy(p, f).wait()
-        forward_y(0, f, u_first[0, f], u_first[1, f])
+        for part in range(parts):
+            window = pl.ds(part * piece, piece)
+            forward_y(0, f, part, u_first[0, f, window, :], u_first[1, f, window, :])
     for i in range(4):
-        table_t[i] = table_ref[i].T
+        flipped = table_ref[i].T
+        table_t[i] = flipped
+        place = 0
+        for s in range(n // 2):
+            for part in range(parts):
+                for p in (0, 1):
+                    first = p * half + s * rows + part * piece
+                    table_x[i, pl.ds(place, piece), :] = flipped[first:first + piece]
+                    place += piece
     factors(0, freq_ref[0, 0])
-    for f in (0, 1):
-        middle(0, f)
+    middle(0, 0)
 
     @pl.when(jnp.logical_not(has_above))
     def _():
@@ -365,12 +404,14 @@
         freq_copy().wait_recv()
         factors(1, freq_in[pl.ds(0, 1), pl.ds(0, 1)])
 
+    middle(0, 1)
     for f in (0, 1):
-        inverse_y(0, f)
-
-        @pl.when(deeper)
-        def _():
-            z_copy(f).start()
+        for part in range(parts):
+            inverse_y(0, f, part)
+
+            @pl.when(deeper)
+            def _():
+                z_copy(f, part).start()
 
     halo_start(0)
 
@@ -378,29 +419,29 @@
     def _():
         inject()
 
+    for part in range(parts):
+        forward_next(0, part)
     halo_wait(0)
     imaging(0)
     image_copy().start()
-
+    middle(1, 0)
+    for part in range(parts):
+        forward_next(1, part)
+    middle(1, 1)
     for f in (0, 1):
-        @pl.when(has_above)
-        def _():
-            z_copy(f).wait_recv()
-
-        forward_y(1, f, u_next[0, f], u_next[1, f])
-    for f in (0, 1):
-        middle(1, f)
-    for f in (0, 1):
-        inverse_y(1, f)
+        for part in range(parts):
+            inverse_y(1, f, part)
     halo_start(1)
     halo_wait(1)
     for f in (0, 1):
         shown_copy(f).start()
+
     for t in range(TICKS):
         for f in (0, 1):
-            for off in order:
-                a2a1_copy(t, f, off).wait_send()
-                a2a2_copy(t, f, off).wait_send()
+            for part in range(parts):
+                for off in order:
+                    a2a1_copy(t, f, part, off).wait_send()
+                    a2a2_copy(t, f, part, off).wait_send()
 
         @pl.when(has_next)
         def _():
@@ -414,7 +455,8 @@
     def _():
         freq_copy().wait_send()
         for f in (0, 1):
-            z_copy(f).wait_send()
+            for part in range(parts):
+                z_copy(f, part).wait_send()
 
     image_copy().wait()
     for f in (0, 1):
@@ -423,29 +465,37 @@
 
 def finish(rows, length, fld_ref, before_ref, out_ref, image_ref, o_sem):
     wide = OFF // 2
+    tiles = length // 128
     step = pl.program_id(0)
     block = image_ref.shape[1]
 
     def out_copy(p, f):
-        return pltpu.make_async_copy(
-            fld_ref.at[p, f, pl.ds(wide, rows), :], out_ref.at[p, :, f, 0, :], o_sem.at[p, f])
+        return [
+            pltpu.make_async_copy(
+                fld_ref.at[p, f, i, pl.ds(wide, rows), :],
+                out_ref.at[p, :, f, 0, pl.ds(i * 128, 128)], o_sem.at[p, f, i])
+            for i in range(tiles)
+        ]
 
     @pl.when(step == 0)
     def _():
         for f in (0, 1):
             for p in (0, 1):
-                out_copy(p, f).start()
+                for copy in out_copy(p, f):
+                    copy.start()
 
     def part(i, carry):
         base = pl.multiple_of(i * 8, 8)
-        window = pl.ds(pl.multiple_of(step * block + base, 8), 8 + 2 * wide)
-        values = [fld_ref[p, f, window, :] for f in (0, 1) for p in (0, 1)]
-        for j in range(OFF):
-            h = j - wide
-            s_real, s_imag = (v[wide - h:wide - h + 8] for v in values[:2])
-            r_real, r_imag = (v[wide + h:wide + h + 8] for v in values[2:])
-            term = s_real * r_real + s_imag * r_imag
-            image_ref[j, pl.ds(base, 8), :] = before_ref[j, pl.ds(base, 8), :] + term
+        top = step * block + base
+        for i_tile in range(tiles):
+            lanes = pl.ds(i_tile * 128, 128)
+            for j in range(OFF):
+                h = j - wide
+                behind, ahead = pl.ds(top + (wide - h), 8), pl.ds(top + (wide + h), 8)
+                term = (
+                    fld_ref[0, 0, i_tile, behind, :] * fld_ref[0, 1, i_tile, ahead, :]
+                    + fld_ref[1, 0, i_tile, behind, :] * fld_ref[1, 1, i_tile, ahead, :])
+                image_ref[j, pl.ds(base, 8), lanes] = before_ref[j, pl.ds(base, 8), lanes] + term
         return carry
 
     lax.fori_loop(0, block // 8, part, 0)
@@ -454,7 +504,8 @@
     def _():
         for f in (0, 1):
             for p in (0, 1):
-                out_copy(p, f).wait()
+                for copy in out_copy(p, f):
+                    copy.wait()
 
 
 def solution(mesh):
@@ -470,11 +521,13 @@
         vmem = pl.BlockSpec(memory_space=pltpu.VMEM)
         smem = pl.BlockSpec(memory_space=pltpu.SMEM)
         f32 = jnp.float32
+        parts = 2 if rows >= 128 else 1
+        tiles = length // 128
         hbm = pl.BlockSpec(memory_space=pl.ANY)
         shown, before = pl.pallas_call(
-            functools.partial(kernel, n, depths, rows, cols, length, nrec),
+            functools.partial(kernel, n, depths, rows, cols, length, nrec, parts),
             out_shape=(
-                jax.ShapeDtypeStruct((2, 2, rows + OFF, length), f32),
+                jax.ShapeDtypeStruct((2, 2, tiles, rows + OFF, 128), f32),
                 jax.ShapeDtypeStruct((OFF, rows, length), f32),
             ),
             in_specs=[smem] * 5 + [hbm] + [vmem] * 4,
@@ -483,21 +536,22 @@
                 pltpu.VMEM((2, 2, rows, length), f32),
                 pltpu.VMEM((OFF, rows, length), f32),
                 pltpu.VMEM((4, length, length), jnp.bfloat16),
-                pltpu.VMEM((2, 2, rows, length), f32),
-                pltpu.VMEM((TICKS, 2, length, 2 * rows), f32),
-                pltpu.VMEM((TICKS, 2, n, cols, 2 * rows), f32),
+                pltpu.VMEM((4, length, length), jnp.bfloat16),
+                pltpu.VMEM((2, 2, tiles, rows, 128), f32),
+                pltpu.VMEM((TICKS, 2, parts, length, 2 * rows // parts), f32),
+                pltpu.VMEM((TICKS, 2, parts, n, cols, 2 * rows // parts), f32),
                 pltpu.VMEM((TICKS, 2, length, 2 * cols), f32),
                 pltpu.VMEM((TICKS, 2, n, rows, 2 * cols), f32),
-                pltpu.VMEM((TICKS, 2, 2, rows + OFF, length), f32),
+                pltpu.VMEM((TICKS, 2, 2, tiles, rows + OFF, 128), f32),
                 pltpu.VMEM((TICKS, 2, cols, length), f32),
                 pltpu.VMEM((TICKS, 2, rows, length), f32),
                 pltpu.VMEM((8, 128), f32),
                 pltpu.VMEM((8, 128), f32),
                 pltpu.VMEM((2 * rows, length), f32),
-                pltpu.SemaphoreType.DMA((TICKS, 2, 2, n)),
-                pltpu.SemaphoreType.DMA((TICKS, 2, 2, n)),
-                pltpu.SemaphoreType.DMA((2,)),
-                pltpu.SemaphoreType.DMA((2,)),
+                pltpu.SemaphoreType.DMA((TICKS, 2, 2, parts, n)),
+                pltpu.SemaphoreType.DMA((TICKS, 2, 2, parts, n)),
+                pltpu.SemaphoreType.DMA((2, parts)),
+                pltpu.SemaphoreType.DMA((2, parts)),
                 pltpu.SemaphoreType.DMA((TICKS, 2)),
                 pltpu.SemaphoreType.DMA((TICKS, 2)),
                 pltpu.SemaphoreType.DMA,
@@ -522,11 +576,11 @@
                 jax.ShapeDtypeStruct((OFF, rows, length), f32),
             ),
             in_specs=[
-                pl.BlockSpec((2, 2, rows + OFF, length), lambda i: (0, 0, 0, 0)),
+                pl.BlockSpec((2, 2, tiles, rows + OFF, 128), lambda i: (0, 0, 0, 0, 0)),
                 pl.BlockSpec((OFF, block, length), lambda i: (0, i, 0)),
             ],
             out_specs=(hbm, pl.BlockSpec((OFF, block, length), lambda i: (0, i, 0))),
-            scratch_shapes=[pltpu.SemaphoreType.DMA((2, 2))],
+            scratch_shapes=[pltpu.SemaphoreType.DMA((2, 2, tiles))],
             compiler_params=pltpu.CompilerParams(vmem_limit_bytes=60 * 2**20),
         )(shown, before)
         return out.reshape(1, 2, rows, 2, 1, length), image[None]

time: 82.5 us -> 83.8 us (1.016)
  the two profiles are of different devices: /device:TPU:13 before, /device:TPU:1 now
where the time goes in v1:
time: 83.8 us; the launch traced here: 83.5 us
  Pallas kernels  80.7 us (96%)
  between operations  2.74 us (3%)
    pallas_call x1, Pallas kernels, local(): pl.pallas_call(functools.partial(kernel, n, depths, rows, cols, length, n...  72.8 us
    pallas_call x1, Pallas kernels, local(): pl.pallas_call(functools.partial(finish, rows, length), grid=(rows // blo...  7.91 us

profile of v1, /device:TPU:1, one launch (start us, length us, event | category | flops | bytes accessed | tf_op | source)
XLA Modules:
  0.0 83.5 jit_solution(10948572715152551956)
XLA Ops:
  2.6 72.8 %shard_map.113 = (f32[2,2,4,144,128]{4,3,2,1,0:T(8,128)}, f32[16,128,512]{2,1,0:T(8,128)}) custom-call(f32[1,1]{1,0:T(1,128)S(6)} %copy.12.freq_ref, f32[1]{0:T(128)S(6)} %copy.13.slow_ref, f32[1,1]{1,0:T(1,128)S(6)} %copy.14.inj_ref, f32[1,2]{1,0:T(1,128)} %bitcast.11, s32[2]{0:T(128)} %src_ref.1, f32[2,128,2,1,512]{4,3,2,1,0:T(1,128)} %bitcast.7, ...), custom_call_target="tpu_custom_call" | custom-call | tf_op jit(solution)/shard_map/pallas_call | solution.py:527
  75.4 7.9 %shard_map.114 = (f32[2,128,2,1,512]{4,3,2,1,0:T(1,128)}, f32[16,128,512]{2,1,0:T(8,128)}) custom-call(f32[2,2,4,144,128]{4,3,2,1,0:T(8,128)} %get-tuple-element.6.fld_ref, f32[16,128,512]{2,1,0:T(8,128)} %get-tuple-element.7.before_ref), custom_call_target="tpu_custom_call" | custom-call | tf_op jit(solution)/shard_map/pallas_call | solution.py:571
